TPU v7x, 32 devices: a whole 2x2x4 slice. The times are simulated.
32 devices in a mesh: groups: 2 (over x), seq: 4 (over y, core), chan: 4 (over z).
Axes of the slice: x: 2, y: 2, z: 4, core: 2. Of those that a mesh axis runs over, the one named last changes fastest.
Arguments:
- dna_act: bfloat16 [6, 2048, 1280], P('groups', 'seq', 'chan'), parts along dimension 0, may hold values from -5 to 5
- conv_weight: bfloat16 [5, 1280, 1536], P(None, 'chan'), may hold values from -0.078125 to 0.078125
- head_weight: bfloat16 [7611, 1536], P(None, 'chan'), may hold values from -0.078125 to 0.078125
- track_ids: int32 [1024], P('groups'), parts along dimension 0, may hold values from 0 to 7610, as said below
- bin_mask: int32 [6, 1024], P('groups', ('seq', 'chan')), parts along dimension 0, may hold values 0 or 1
- counts: int32 [6, 1024, 512], P('groups', ('seq', 'chan')), parts along dimension 0, may hold values from 0 to 3
Outputs:
- grad_input: bfloat16 [6, 2048, 1280], P('groups', 'seq', 'chan'), parts along dimension 0
- grad_conv: float32 [10, 1280, 1536], P('groups', 'chan', 'seq'), parts along dimension 0
- grad_tracks: float32 [1024, 1536], P(('groups', 'seq'), 'chan'), parts along dimension 0
There are 2 independent parts, one for each index of `groups`. A program takes and returns all parts, laid end to end along the dimension named above; an argument that names none is the same for every part. Nothing has to cross between parts.
Inputs may be any that keep to these rules, and one draw needn't show every extreme that they name: `track_ids`: the 512 track numbers are distinct.
All inputs are finite; a program needn't handle non-finite values. No bound on the sum of `bin_mask` on one device may be relied on, other than what follows from the above.
Results may differ from a plain program's by a relative error of at most 0.011.
Values may be sent and summed in bfloat16 or wider, within the bound.
No kernel may reach another device: no remote copies, remote signals or barrier semaphores. Data moves between devices by JAX's collectives and lax.ppermute only.
A program may use at most 128 MiB of HBM per device.

v0:
```python
import jax
import jax.numpy as jnp
from jax import lax
from jax.sharding import PartitionSpec as P

KSIZE = 5


def padded_2(cells, sides, width):
    for axis, dim in sides:
        count = lax.axis_size(axis)
        ends = count - 1
        head = lax.slice_in_dim(cells, 0, width, axis=dim)
        tail = lax.slice_in_dim(cells, cells.shape[dim] - width, cells.shape[dim], axis=dim)
        cells = jnp.concatenate(
            [
                lax.ppermute(tail, axis, [(i, (i + 1) % count) for i in range(ends)]),
                cells,
                lax.ppermute(head, axis, [((i + 1) % count, i) for i in range(ends)]),
            ],
            axis=dim,
        )
    return cells


def exact_gelu(values):
    return jax.nn.gelu(values, approximate=False)


def local(dna_act, conv_weight, head_weight, track_ids, bin_mask, counts):
    seq_count, positions, channels = dna_act.shape
    out_width = conv_weight.shape[2]
    gelu_out, gelu_back = jax.vjp(exact_gelu, dna_act.astype(jnp.float32))
    activated = gelu_out.astype(jnp.bfloat16)
    padded = padded_2(activated, (("seq", 1),), 2)
    windows = jnp.concatenate(
        [padded[:, offset : offset + positions] for offset in range(KSIZE)], axis=2
    )
    flat_weight = conv_weight.reshape(KSIZE * channels, out_width)
    conv_part = jnp.einsum("stj,jo->sto", windows, flat_weight, preferred_element_type=jnp.float32)
    pooled_part = conv_part.reshape(seq_count, positions // 2, 2, out_width).sum(axis=2) * 0.5
    bin_rows = lax.psum_scatter(
        pooled_part.astype(jnp.bfloat16), "chan", scatter_dimension=1, tiled=True
    )
    local_rows = jnp.take(head_weight, track_ids, axis=0)
    chosen = lax.all_gather(local_rows, "chan", axis=1, tiled=True)
    logits = jnp.einsum("snd,md->snm", bin_rows, chosen, preferred_element_type=jnp.float32)
    mask_column = bin_mask.astype(jnp.float32)[:, :, None]
    grad_logit = (mask_column * (jnp.exp(logits) - counts.astype(jnp.float32))).astype(jnp.bfloat16)
    grad_bins = jnp.einsum(
        "snm,md->snd", grad_logit, chosen, preferred_element_type=jnp.float32
    ).astype(jnp.bfloat16)
    slab_grad = lax.all_gather(grad_bins, "chan", axis=1, tiled=True)
    track_part = jnp.einsum("snm,snd->md", grad_logit, bin_rows, preferred_element_type=jnp.float32)
    track_summed = lax.psum_scatter(
        track_part.astype(jnp.bfloat16), "seq", scatter_dimension=0, tiled=True
    )
    grad_tracks = lax.psum_scatter(track_summed, "chan", scatter_dimension=1, tiled=True).astype(
        jnp.float32
    )
    rim_grad = padded_2(slab_grad, (("seq", 1),), 1)
    wide_grad = jnp.repeat(rim_grad, 2, axis=1) * 0.5
    projected = jnp.einsum(
        "sqo,jo->sqj", wide_grad, flat_weight, preferred_element_type=jnp.float32
    )
    projected = projected.reshape(seq_count, positions + 4, KSIZE, channels)
    grad_acts = projected[:, 4 : 4 + positions, 0]
    for offset in range(1, KSIZE):
        grad_acts = grad_acts + projected[:, 4 - offset : 4 - offset + positions, offset]
    grad_input = gelu_back(grad_acts)[0].astype(jnp.bfloat16)
    slab_upsampled = jnp.repeat(slab_grad, 2, axis=1) * 0.5
    flat_grad = jnp.einsum(
        "stj,sto->jo", windows, slab_upsampled, preferred_element_type=jnp.float32
    )
    grad_conv = lax.psum_scatter(
        flat_grad.reshape(KSIZE, channels, out_width).astype(jnp.bfloat16),
        "seq",
        scatter_dimension=2,
        tiled=True,
    ).astype(jnp.float32)
    return (grad_input, grad_conv, grad_tracks)


def solution(mesh):
    in_specs = (
        P("groups", "seq", "chan"),
        P(None, "chan", None),
        P(None, "chan"),
        P("groups"),
        P("groups", ("seq", "chan")),
        P("groups", ("seq", "chan"), None),
    )
    out_specs = (
        P("groups", "seq", "chan"),
        P("groups", "chan", "seq"),
        P(("groups", "seq"), "chan"),
    )
    return jax.shard_map(local, mesh=mesh, in_specs=in_specs, out_specs=out_specs, check_vma=False)
```

profile of v0, /device:TPU:0, one launch (start us, length us, event | category | flops | bytes accessed | tf_op | source)
XLA Modules:
  0.0 317.8 jit_solution(13602244970949401829)
XLA Ops:
  8.9 6.0 %fusion.12 = (bf16[3,512,320]{2,1,0:T(8,128)(2,1)S(1)}, f32[3,512,320]{2,1,0:T(8,128)}) fusion(bf16[3,512,320]{2,1,0:T(8,128)(2,1)S(1)} %copy.17), kind=kLoop, calls=%fused_computation.19 | loop fusion | flops 32440320 | bytes 3932160 | tf_op jit(solution)/shard_map/convert_element_type | solution.py:34
  15.0 2.4 collective-permute-start
  18.7 5.2 %gather_fusion = bf16[512,384]{1,0:T(8,128)(2,1)S(1)} fusion(bf16[7611,384]{1,0:T(8,128)(2,1)} %param.8, s32[1024]{0:T(1024)S(1)} %pad_clamp_fusion), kind=kCustom, calls=%fused_computation | custom fusion | bytes 788480 | tf_op jit(solution)/shard_map/jit(_take)/gather | solution.py:45
  24.9 3.4 %pad_maximum_fusion = (bf16[3,512,320]{2,1,0:T(8,128)(2,1)S(1)}, bf16[3,512,320]{2,1,0:T(8,128)(2,1)}, bf16[3,512,320]{2,1,0:T(8,128)(2,1)}, bf16[3,512,320]{2,1,0:T(8,128)(2,1)}) fusion(bf16[3,2,320]{2,1,0:T(2,128)(2,1)S(1)} %collective-permute-done.1, bf16[3,512,320]{2,1,0:T(8,128)(2,1)S(1)} %get-tuple-element.12, ...), kind=kLoop, calls=%fused_computation.71 | loop fusion | flops 7864320 | bytes 4922880 | tf_op jit(solution)/shard_map/concatenate | solution.py:15
  28.3 9.0 %concatenate.17 = bf16[3,512,1600]{2,1,0:T(8,128)(2,1)} concatenate(bf16[3,512,320]{2,1,0:T(8,128)(2,1)} %get-tuple-element.20, bf16[3,512,320]{2,1,0:T(8,128)(2,1)} %get-tuple-element.21, bf16[3,512,320]{2,1,0:T(8,128)(2,1)S(1)} %get-tuple-element.12, bf16[3,512,320]{2,1,0:T(8,128)(2,1)} %get-tuple-element.17, bf16[3,512,320]{2,1,0:T(8,128)(2,1)S(1)} %get-tuple-element.16), dimensions={2} | concatenate | bytes 9830400 | tf_op jit(solution)/shard_map/concatenate | solution.py:36
  37.3 11.0 %dot_general.24 = bf16[3,256,2,1600]{3,2,1,0:T(2,128)(2,1)} reshape(bf16[3,512,1600]{2,1,0:T(8,128)(2,1)} %concatenate.17) | data formatting | bytes 9830400 | tf_op jit(solution)/shard_map/stj,jo->sto/dot_general | solution.py:40
  48.3 12.4 %fusion.7 = f32[3,256,1536]{2,1,0:T(8,128)S(1)} fusion(bf16[1600,1536,1,1]{1,0,3,2:T(8,128)(2,1)} %bitcast.55, bf16[3,256,2,1600]{3,2,1,0:T(2,128)(2,1)} %dot_general.24), kind=kOutput, calls=%fused_computation.14 | convolution fusion | flops 7550926848 | bytes 14548992 | tf_op jit(solution)/shard_map/stj,jo->sto/dot_general | solution.py:40
  60.7 2.1 multiply_convert_fusion
  63.5 2.7 all-gather.3.cloned.1.call-done
  66.2 49.4 %reduce-scatter.9.cloned.1.call-done = bf16[3,64,1536]{2,1,0:T(8,128)(2,1)} async-done(((bf16[3,256,1536]{2,1,0:T(8,128)(2,1)}), bf16[3,64,1536]{2,1,0:T(8,128)(2,1)}) %reduce-scatter.9.cloned.1.call-update) | async-done | bytes 589840 | tf_op jit(solution)/shard_map/reduce_scatter | solution.py:42
  115.6 2.3 fusion.62
  119.8 2.7 convolution_convert_fusion
  122.7 7.8 %copy.19 = bf16[1600,3,512]{2,0,1:T(8,128)(2,1)} copy(bf16[1600,3,512]{0,2,1:T(8,128)(2,1)} %bitcast.49) | data formatting | bytes 9830400 | tf_op jit(solution)/shard_map/stj,sto->jo/dot_general | solution.py:72
  130.5 16.8 %reduce-scatter.11.cloned.1.call-done = bf16[128,1536]{1,0:T(8,128)(2,1)} async-done(((bf16[512,1536]{1,0:T(8,128)(2,1)}), bf16[128,1536]{1,0:T(8,128)(2,1)}) %reduce-scatter.11.cloned.1.call-update) | async-done | bytes 393232 | tf_op jit(solution)/shard_map/reduce_scatter | solution.py:55
  147.3 1.9 copy.26
  149.3 50.0 %all-gather.5.cloned.1.call-done = bf16[3,256,1536]{2,1,0:T(8,128)(2,1)} async-done(((bf16[3,64,1536]{2,1,0:T(8,128)(2,1)}), bf16[3,256,1536]{2,1,0:T(8,128)(2,1)}) %all-gather.5.cloned.1.call-update) | async-done | bytes 2359312 | tf_op jit(solution)/shard_map/all_gather | solution.py:53
  199.3 1.9 broadcast_multiply_fusion
  201.2 4.0 %broadcast_in_dim.23 = bf16[3,256,2,1536]{3,2,1,0:T(2,128)(2,1)} broadcast(bf16[3,256,1536]{2,1,0:T(8,128)(2,1)S(1)} %broadcast_multiply_fusion), dimensions={0,1,3} | broadcast | bytes 7077888 | tf_op jit(solution)/shard_map/broadcast_in_dim | solution.py:71
  205.2 10.7 %reshape.44 = bf16[3,512,1536,1]{2,1,0,3:T(8,128)(2,1)} reshape(bf16[3,256,2,1536]{3,2,1,0:T(2,128)(2,1)} %broadcast_in_dim.23) | data formatting | bytes 9437184 | tf_op jit(solution)/shard_map/mul | solution.py:71
  215.9 12.5 %bitcast_convert_fusion = bf16[5,320,1536]{2,1,0:T(8,128)(2,1)} fusion(bf16[5,320,3,512]{3,1,0,2:T(8,128)(2,1)} %bitcast.52, bf16[3,512,1536,1]{2,1,0,3:T(8,128)(2,1)} %reshape.44), kind=kOutput, calls=%fused_computation.1 | convolution fusion | flops 7552204800 | bytes 14548992 | tf_op jit(solution)/shard_map/stj,sto->jo/dot_general | solution.py:72
  228.5 11.7 %copy.24 = bf16[5,320,1536]{1,0,2:T(8,128)(2,1)} copy(bf16[5,320,1536]{2,1,0:T(8,128)(2,1)} %bitcast_convert_fusion) | data formatting | bytes 9830400
  240.2 12.8 %reshape.49 = bf16[1536,1600]{1,0:T(8,128)(2,1)} reshape(bf16[1536,5,320]{2,1,0:T(8,128)(2,1)} %bitcast.50) | data formatting | bytes 9830400
  256.9 3.2 collective-permute-done.3
  260.0 3.2 %maximum_multiply_fusion = bf16[3,258,1536]{2,1,0:T(8,128)(2,1)S(1)} fusion(bf16[3,1,1536]{2,1,0:T(2,128)(2,1)S(1)} %collective-permute-done.3, bf16[3,256,1536]{2,1,0:T(8,128)(2,1)} %all-gather.5.cloned.1.call-done, bf16[3,1,1536]{2,1,0:T(2,128)(2,1)S(1)} %collective-permute-done.2), kind=kLoop, calls=%fused_computation.18 | loop fusion | flops 9510912 | bytes 4755456 | tf_op jit(solution)/shard_map/mul | solution.py:62
  263.2 4.3 %broadcast_in_dim.22 = bf16[3,258,2,1536]{3,2,1,0:T(2,128)(2,1)} broadcast(bf16[3,258,1536]{2,1,0:T(8,128)(2,1)S(1)} %maximum_multiply_fusion), dimensions={0,1,3} | broadcast | bytes 7133184 | tf_op jit(solution)/shard_map/broadcast_in_dim | solution.py:62
  267.5 6.4 %reshape.42 = bf16[3,516,1536,1]{2,1,0,3:T(8,128)(2,1)} reshape(bf16[3,258,2,1536]{3,2,1,0:T(2,128)(2,1)} %broadcast_in_dim.22) | data formatting | bytes 9510912 | tf_op jit(solution)/shard_map/mul | solution.py:62
  273.9 14.4 %fusion.2 = f32[3,516,5,320]{3,1,2,0:T(8,128)S(1)} fusion(bf16[5,320,1536]{2,1,0:T(8,128)(2,1)} %param.7, bf16[3,516,1536,1]{2,1,0,3:T(8,128)(2,1)} %reshape.42), kind=kOutput, calls=%fused_computation.4 | convolution fusion | flops 7608729600 | bytes 19577856 | tf_op jit(solution)/shard_map/sqo,jo->sqj/dot_general | solution.py:63
  288.4 2.1 fusion.18
  293.6 8.8 %reduce-scatter.13.cloned.1.call-done = bf16[384,1600]{1,0:T(8,128)(2,1)} async-done(((bf16[1536,1600]{1,0:T(8,128)(2,1)}), bf16[384,1600]{1,0:T(8,128)(2,1)}) %reduce-scatter.13.cloned.1.call-update) | async-done | bytes 1228816
  302.4 3.3 %reshape.50 = bf16[384,5,320]{2,1,0:T(8,128)(2,1)S(1)} reshape(bf16[384,1600]{1,0:T(8,128)(2,1)} %reduce-scatter.13.cloned.1.call-done) | data formatting | bytes 2457600
  305.6 2.4 copy.25
  308.0 2.9 convert_element_type.45
  (41 shorter events, 13.7 us)
Async XLA Ops:
  7.2 59.0 %all-gather.3.cloned.1.call-start = ((), (), s32[]{:S(2)}) async-start(), calls=%async_computation.5 | async-start | bytes 1966080 | tf_op jit(solution)/shard_map/all_gather | solution.py:46
  8.9 9.8 %copy-start.3 = (s32[512]{0:T(512)S(1)}, s32[512]{0:T(512)}, u32[]{:S(2)}) copy-start(s32[512]{0:T(512)} %param.9) | copy-start | bytes 6148
  15.0 10.0 %collective-permute-start = (bf16[3,2,320]{2,1,0:T(2,128)(2,1)S(1)}, bf16[3,2,320]{2,1,0:T(2,128)(2,1)S(1)}, u32[]{:S(2)}, u32[]{:S(2)}) collective-permute-start(bf16[3,2,320]{2,1,0:T(2,128)(2,1)S(1)} %get-tuple-element.23), channel_id=1, source_target_pairs={{0,4},{4,8},{8,12},{1,5},{5,9},{9,13},{2,6},{6,10},{10,14},{3,7},{... | collective-permute-start | bytes 11528 | tf_op jit(solution)/shard_map/ppermute | solution.py:17
  17.4 7.6 %collective-permute-start.1 = (bf16[3,2,320]{2,1,0:T(2,128)(2,1)S(1)}, bf16[3,2,320]{2,1,0:T(2,128)(2,1)S(1)}, u32[]{:S(2)}, u32[]{:S(2)}) collective-permute-start(bf16[3,2,320]{2,1,0:T(2,128)(2,1)S(1)} %get-tuple-element.22), channel_id=1, source_target_pairs={{4,0},{8,4},{12,8},{5,1},{9,5},{13,9},{6,2},{10,6},{14,10},{7,3},{... | collective-permute-start | bytes 11528 | tf_op jit(solution)/shard_map/ppermute | solution.py:19
  24.9 90.7 %reduce-scatter.9.cloned.1.call-start = ((), (), s32[]{:S(2)}) async-start(), calls=%async_computation.4 | async-start | bytes 2949120 | tf_op jit(solution)/shard_map/reduce_scatter | solution.py:42
  62.8 0.7 copy-start.4
  62.8 52.8 %copy-start.2 = (s32[3,64,512]{2,1,0:T(8,128)S(1)}, s32[3,64,512]{2,1,0:T(8,128)}, u32[]{:S(2)}) copy-start(s32[3,64,512]{2,1,0:T(8,128)} %param.11) | copy-start | bytes 1179652
  62.8 84.5 %reduce-scatter.11.cloned.1.call-start = ((), (), s32[]{:S(2)}) async-start(), calls=%async_computation.7 | async-start | bytes 1966080 | tf_op jit(solution)/shard_map/reduce_scatter | solution.py:55
  115.6 2.3 copy-start.1
  119.7 79.6 %all-gather.5.cloned.1.call-start = ((), (), s32[]{:S(2)}) async-start(), calls=%async_computation.6 | async-start | bytes 2949120 | tf_op jit(solution)/shard_map/all_gather | solution.py:53
  122.5 169.4 %reduce-scatter.15.cloned.1.call-start = ((), (), s32[]{:S(2)}) async-start(), calls=%async_computation.9 | async-start | bytes 491520
  149.2 153.1 %reduce-scatter.13.cloned.1.call-start = ((), (), s32[]{:S(2)}) async-start(), calls=%async_computation.8 | async-start | bytes 6389760
  254.0 2.9 collective-permute-start.2
  255.5 4.5 %collective-permute-start.3 = (bf16[3,1,1536]{2,1,0:T(2,128)(2,1)S(1)}, bf16[3,1,1536]{2,1,0:T(2,128)(2,1)S(1)}, u32[]{:S(2)}, u32[]{:S(2)}) collective-permute-start(bf16[3,1,1536]{2,1,0:T(2,128)(2,1)S(1)} %get-tuple-element.15), channel_id=1, source_target_pairs={{4,0},{8,4},{12,8},{5,1},{9,5},{13,9},{6,2},{10,6},{14,10},{7,3},{... | collective-permute-start | bytes 27656 | tf_op jit(solution)/shard_map/ppermute | solution.py:19
  273.9 14.4 %copy-start = (f32[3,512,320]{2,1,0:T(8,128)S(1)}, f32[3,512,320]{2,1,0:T(8,128)}, u32[]{:S(2)}) copy-start(f32[3,512,320]{2,1,0:T(8,128)} %get-tuple-element.13) | copy-start | bytes 5898244
Sparse Core Ops, SparseCore 0:
  25.0 41.1 all-gather.2
  68.5 47.0 reduce-scatter.8
  119.8 27.4 reduce-scatter.10
  149.3 49.9 all-gather.4
  201.4 19.4 reduce-scatter.14
  253.1 49.2 reduce-scatter.12
where the time goes:
time: 320 us; the launch traced here: 318 us
  waiting for transfers between devices  131 us (41%)
  local copies, waits for them, and re-layouts  96.2 us (30%)
  matrix products  46.1 us (14%)
  other arithmetic  23.2 us (7%)
  between operations  14.3 us (4%)
  starting transfers between devices  6.99 us (2%)
    all_gather x1, waiting for transfers between devices, local(): slab_grad = lax.all_gather(grad_bins, 'chan', axis=1, tiled=True)  50 us
    reduce_scatter x1, waiting for transfers between devices, local(): lax.psum_scatter(pooled_part.astype(jnp.bfloat16), 'chan', scatter_dimens...  49.4 us
    unnamed x18, local copies, waits for them, and re-layouts  36.8 us
    reduce_scatter x1, waiting for transfers between devices, local(): lax.psum_scatter(track_part.astype(jnp.bfloat16), 'seq', scatter_dimensio...  16.8 us
    dot_general x1, matrix products, local(): jnp.einsum('sqo,jo->sqj', wide_grad, flat_weight, preferred_element_type=...  14.4 us
    dot_general x1, matrix products, local(): jnp.einsum('stj,sto->jo', windows, slab_upsampled, preferred_element_type...  12.5 us
    dot_general x1, matrix products, local(): jnp.einsum('stj,jo->sto', windows, flat_weight, preferred_element_type=jn...  12.4 us
    dot_general x1, local copies, waits for them, and re-layouts, local(): jnp.einsum('stj,jo->sto', windows, flat_weight, preferred_element_type=jn...  11 us
  transfers between devices with their start and end apart: 10, of which 6 were waited for; matrix products, arithmetic and copies ran while one was open for 46% of the time, Pallas kernels for 0%

commit v1 on v0

--- a/solution.py
+++ b/solution.py
@@ -4,6 +4,23 @@
 from jax.sharding import PartitionSpec as P
 
 KSIZE = 5
+
+
+def in_order(tiles, dim):
+    shape = list(tiles.shape[1:])
+    shape[dim] *= tiles.shape[0]
+    return jnp.moveaxis(tiles, 0, dim).reshape(shape)
+
+
+def grow_blocks(x, axis):
+    size, position = (lax.axis_size(axis), lax.axis_index(axis))
+    tiles, bit = (x[None], 1)
+    while bit < size:
+        other = lax.ppermute(tiles, axis, [(i, i ^ bit) for i in range(size)])
+        low = position & bit == 0
+        tiles = jnp.concatenate([jnp.where(low, tiles, other), jnp.where(low, other, tiles)])
+        bit *= 2
+    return tiles
 
 
 def padded_2(cells, sides, width):
@@ -50,7 +67,7 @@
     grad_bins = jnp.einsum(
         "snm,md->snd", grad_logit, chosen, preferred_element_type=jnp.float32
     ).astype(jnp.bfloat16)
-    slab_grad = lax.all_gather(grad_bins, "chan", axis=1, tiled=True)
+    slab_grad = in_order(grow_blocks(grad_bins, "chan"), 1)
     track_part = jnp.einsum("snm,snd->md", grad_logit, bin_rows, preferred_element_type=jnp.float32)
     track_summed = lax.psum_scatter(
         track_part.astype(jnp.bfloat16), "seq", scatter_dimension=0, tiled=True

time: 320 us -> 310 us (0.969)
  waiting for transfers between devices: 131 us -> 120 us
  starting transfers between devices: 6.99 us -> 10.4 us
    ppermute x0 -> x2, waiting for transfers between devices: none -> 53.7 us  [grow_blocks(): other = lax.ppermute(tiles, axis, [(i, i ^ bit) for i in range(size)])]
    all_gather x1 -> x0, waiting for transfers between devices: 50 us -> none  [local(): slab_grad = lax.all_gather(grad_bins, 'chan', axis=1, tiled=True)]
    reduce_scatter x1, waiting for transfers between devices: 16.8 us -> 0.01 us  [local(): lax.psum_scatter(track_part.astype(jnp.bfloat16), 'seq', scatter_dimensio...]
    unnamed x8 -> x7, waiting for transfers between devices: 8.85 us -> 12.4 us
  transfers between devices with their start and end apart: 10 -> 11, of which waited for: 6 -> 6; matrix products, arithmetic and copies ran while one was open for 46% -> 46% of each run, Pallas kernels for 0% -> 0%
where the time goes in v1:
time: 310 us; the launch traced here: 308 us
  waiting for transfers between devices  120 us (39%)
  local copies, waits for them, and re-layouts  95.2 us (31%)
  matrix products  45.9 us (15%)
  other arithmetic  22.1 us (7%)
  between operations  14 us (5%)
  starting transfers between devices  10.4 us (3%)
    ppermute x2, waiting for transfers between devices, grow_blocks(): other = lax.ppermute(tiles, axis, [(i, i ^ bit) for i in range(size)])  53.7 us
    reduce_scatter x1, waiting for transfers between devices, local(): lax.psum_scatter(pooled_part.astype(jnp.bfloat16), 'chan', scatter_dimens...  49.4 us
    unnamed x18, local copies, waits for them, and re-layouts  36.8 us
    dot_general x1, matrix products, local(): jnp.einsum('sqo,jo->sqj', wide_grad, flat_weight, preferred_element_type=...  15.3 us
    dot_general x1, matrix products, local(): jnp.einsum('stj,sto->jo', windows, slab_upsampled, preferred_element_type...  12.6 us
    dot_general x1, matrix products, local(): jnp.einsum('stj,jo->sto', windows, flat_weight, preferred_element_type=jn...  12.4 us
    unnamed x7, waiting for transfers between devices  12.4 us
    dot_general x1, local copies, waits for them, and re-layouts, local(): jnp.einsum('stj,jo->sto', windows, flat_weight, preferred_element_type=jn...  10.9 us
  transfers between devices with their start and end apart: 11, of which 6 were waited for; matrix products, arithmetic and copies ran while one was open for 46% of the time, Pallas kernels for 0%

profile of v1, /device:TPU:0, one launch (start us, length us, event | category | flops | bytes accessed | tf_op | source)
XLA Modules:
  0.0 307.7 jit_solution(5509166491885590935)
XLA Ops:
  7.2 1.7 copy.18
  8.9 6.0 %fusion.13 = (bf16[3,512,320]{2,1,0:T(8,128)(2,1)S(1)}, f32[3,512,320]{2,1,0:T(8,128)}) fusion(bf16[3,512,320]{2,1,0:T(8,128)(2,1)S(1)} %copy.18), kind=kLoop, calls=%fused_computation.20 | loop fusion | flops 32440320 | bytes 3932160 | tf_op jit(solution)/shard_map/convert_element_type | solution.py:51
  16.3 3.0 collective-permute-start
  19.3 5.2 %gather_fusion = bf16[512,384]{1,0:T(8,128)(2,1)S(1)} fusion(bf16[7611,384]{1,0:T(8,128)(2,1)} %param.8, s32[1024]{0:T(1024)S(1)} %pad_clamp_fusion), kind=kCustom, calls=%fused_computation | custom fusion | bytes 788480 | tf_op jit(solution)/shard_map/jit(_take)/gather | solution.py:62
  25.6 3.4 %pad_maximum_fusion = (bf16[3,512,320]{2,1,0:T(8,128)(2,1)S(1)}, bf16[3,512,320]{2,1,0:T(8,128)(2,1)}, bf16[3,512,320]{2,1,0:T(8,128)(2,1)}, bf16[3,512,320]{2,1,0:T(8,128)(2,1)}) fusion(bf16[3,2,320]{2,1,0:T(2,128)(2,1)S(1)} %collective-permute-done.1, bf16[3,512,320]{2,1,0:T(8,128)(2,1)S(1)} %get-tuple-element.12, ...), kind=kLoop, calls=%fused_computation.73 | loop fusion | flops 7864320 | bytes 4922880 | tf_op jit(solution)/shard_map/concatenate | solution.py:32
  28.9 9.0 %concatenate.23 = bf16[3,512,1600]{2,1,0:T(8,128)(2,1)} concatenate(bf16[3,512,320]{2,1,0:T(8,128)(2,1)} %get-tuple-element.24, bf16[3,512,320]{2,1,0:T(8,128)(2,1)} %get-tuple-element.25, bf16[3,512,320]{2,1,0:T(8,128)(2,1)S(1)} %get-tuple-element.12, bf16[3,512,320]{2,1,0:T(8,128)(2,1)} %get-tuple-element.19, bf16[3,512,320]{2,1,0:T(8,128)(2,1)S(1)} %get-tuple-element.18), dimensions={2} | concatenate | bytes 9830400 | tf_op jit(solution)/shard_map/concatenate | solution.py:53
  37.9 10.9 %dot_general.24 = bf16[3,256,2,1600]{3,2,1,0:T(2,128)(2,1)} reshape(bf16[3,512,1600]{2,1,0:T(8,128)(2,1)} %concatenate.23) | data formatting | bytes 9830400 | tf_op jit(solution)/shard_map/stj,jo->sto/dot_general | solution.py:57
  48.8 12.4 %fusion.7 = f32[3,256,1536]{2,1,0:T(8,128)S(1)} fusion(bf16[1600,1536,1,1]{1,0,3,2:T(8,128)(2,1)} %bitcast.63, bf16[3,256,2,1600]{3,2,1,0:T(2,128)(2,1)} %dot_general.24), kind=kOutput, calls=%fused_computation.14 | convolution fusion | flops 7550926848 | bytes 14548992 | tf_op jit(solution)/shard_map/stj,jo->sto/dot_general | solution.py:57
  61.2 2.0 multiply_convert_fusion
  65.0 49.4 %reduce-scatter.9.cloned.1.call-done = bf16[3,64,1536]{2,1,0:T(8,128)(2,1)} async-done(((bf16[3,256,1536]{2,1,0:T(8,128)(2,1)}), bf16[3,64,1536]{2,1,0:T(8,128)(2,1)}) %reduce-scatter.9.cloned.1.call-update) | async-done | bytes 589840 | tf_op jit(solution)/shard_map/reduce_scatter | solution.py:59
  114.3 2.3 fusion.63
  118.0 2.8 fusion.6
  121.1 10.9 %collective-permute-done.2 = bf16[1,3,64,1536]{3,2,1,0:T(8,128)(2,1)} collective-permute-done((bf16[1,3,64,1536]{3,2,1,0:T(8,128)(2,1)S(1)}, bf16[1,3,64,1536]{3,2,1,0:T(8,128)(2,1)}, u32[]{:S(2)}, u32[]{:S(2)}) %collective-permute-start.2) | collective-permute-done | bytes 589856 | tf_op jit(solution)/shard_map/ppermute | solution.py:19
  133.2 2.2 collective-permute-start.3
  135.4 7.7 %copy.21 = bf16[1600,3,512]{2,0,1:T(8,128)(2,1)} copy(bf16[1600,3,512]{0,2,1:T(8,128)(2,1)} %bitcast.55) | data formatting | bytes 9830400 | tf_op jit(solution)/shard_map/stj,sto->jo/dot_general | solution.py:89
  143.2 42.9 %collective-permute-done.3 = bf16[2,3,64,1536]{3,2,1,0:T(8,128)(2,1)} collective-permute-done((bf16[2,3,64,1536]{3,2,1,0:T(8,128)(2,1)S(1)}, bf16[2,3,64,1536]{3,2,1,0:T(8,128)(2,1)}, u32[]{:S(2)}, u32[]{:S(2)}) %collective-permute-start.3) | collective-permute-done | bytes 1179680 | tf_op jit(solution)/shard_map/ppermute | solution.py:19
  186.0 1.4 broadcast_select_fusion.1
  188.2 4.0 %broadcast_in_dim.27 = bf16[3,256,2,1536]{3,2,1,0:T(2,128)(2,1)} broadcast(bf16[3,256,1536]{2,1,0:T(8,128)(2,1)S(1)} %broadcast_multiply_fusion), dimensions={0,1,3} | broadcast | bytes 7077888 | tf_op jit(solution)/shard_map/broadcast_in_dim | solution.py:88
  192.2 10.7 %reshape.48 = bf16[3,512,1536,1]{2,1,0,3:T(8,128)(2,1)} reshape(bf16[3,256,2,1536]{3,2,1,0:T(2,128)(2,1)} %broadcast_in_dim.27) | data formatting | bytes 9437184 | tf_op jit(solution)/shard_map/mul | solution.py:88
  202.9 1.9 copy.28
  204.9 12.6 %bitcast_convert_fusion = bf16[5,320,1536]{2,1,0:T(8,128)(2,1)} fusion(bf16[5,320,3,512]{3,1,0,2:T(8,128)(2,1)} %bitcast.60, bf16[3,512,1536,1]{2,1,0,3:T(8,128)(2,1)} %reshape.48), kind=kOutput, calls=%fused_computation.1 | convolution fusion | flops 7552204800 | bytes 14548992 | tf_op jit(solution)/shard_map/stj,sto->jo/dot_general | solution.py:89
  217.5 11.7 %copy.26 = bf16[5,320,1536]{1,0,2:T(8,128)(2,1)} copy(bf16[5,320,1536]{2,1,0:T(8,128)(2,1)} %bitcast_convert_fusion) | data formatting | bytes 9830400
  229.2 12.8 %reshape.53 = bf16[1536,1600]{1,0:T(8,128)(2,1)} reshape(bf16[1536,5,320]{2,1,0:T(8,128)(2,1)} %bitcast.56) | data formatting | bytes 9830400
  244.7 3.6 %collective-permute-done.5 = bf16[3,1,1536]{2,1,0:T(2,128)(2,1)S(1)} collective-permute-done((bf16[3,1,1536]{2,1,0:T(2,128)(2,1)S(1)}, bf16[3,1,1536]{2,1,0:T(2,128)(2,1)S(1)}, u32[]{:S(2)}, u32[]{:S(2)}) %collective-permute-start.5) | collective-permute-done | bytes 9248 | tf_op jit(solution)/shard_map/ppermute | solution.py:36
  249.0 4.3 %broadcast_in_dim.26 = bf16[3,258,2,1536]{3,2,1,0:T(2,128)(2,1)} broadcast(bf16[3,258,1536]{2,1,0:T(8,128)(2,1)S(1)} %maximum_multiply_fusion), dimensions={0,1,3} | broadcast | bytes 7133184 | tf_op jit(solution)/shard_map/broadcast_in_dim | solution.py:79
  253.2 6.5 %reshape.46 = bf16[3,516,1536,1]{2,1,0,3:T(8,128)(2,1)} reshape(bf16[3,258,2,1536]{3,2,1,0:T(2,128)(2,1)} %broadcast_in_dim.26) | data formatting | bytes 9510912 | tf_op jit(solution)/shard_map/mul | solution.py:79
  259.7 15.3 %fusion.2 = f32[3,516,5,320]{3,1,2,0:T(8,128)S(1)} fusion(bf16[5,320,1536]{2,1,0:T(8,128)(2,1)} %param.7, bf16[3,516,1536,1]{2,1,0,3:T(8,128)(2,1)} %reshape.46), kind=kOutput, calls=%fused_computation.4 | convolution fusion | flops 7608729600 | bytes 19577856 | tf_op jit(solution)/shard_map/sqo,jo->sqj/dot_general | solution.py:80
  275.0 2.1 fusion.19
  280.3 12.3 %reduce-scatter.13.cloned.1.call-done = bf16[384,1600]{1,0:T(8,128)(2,1)} async-done(((bf16[1536,1600]{1,0:T(8,128)(2,1)}), bf16[384,1600]{1,0:T(8,128)(2,1)}) %reduce-scatter.13.cloned.1.call-update) | async-done | bytes 1228816
  292.6 3.3 %reshape.54 = bf16[384,5,320]{2,1,0:T(8,128)(2,1)S(1)} reshape(bf16[384,1600]{1,0:T(8,128)(2,1)} %reduce-scatter.13.cloned.1.call-done) | data formatting | bytes 2457600
  295.8 2.4 copy.27
  298.2 2.9 convert_element_type.45
  (47 shorter events, 14.1 us)
Async XLA Ops:
  7.2 57.8 %all-gather.2.cloned.1.call-start = ((), (), s32[]{:S(2)}) async-start(), calls=%async_computation.5 | async-start | bytes 1966080 | tf_op jit(solution)/shard_map/all_gather | solution.py:63
  8.9 10.4 %copy-start.3 = (s32[512]{0:T(512)S(1)}, s32[512]{0:T(512)}, u32[]{:S(2)}) copy-start(s32[512]{0:T(512)} %param.9) | copy-start | bytes 6148
  15.0 10.6 %collective-permute-start.1 = (bf16[3,2,320]{2,1,0:T(2,128)(2,1)S(1)}, bf16[3,2,320]{2,1,0:T(2,128)(2,1)S(1)}, u32[]{:S(2)}, u32[]{:S(2)}) collective-permute-start(bf16[3,2,320]{2,1,0:T(2,128)(2,1)S(1)} %get-tuple-element.26), channel_id=1, source_target_pairs={{4,0},{8,4},{12,8},{5,1},{9,5},{13,9},{6,2},{10,6},{14,10},{7,3},{... | collective-permute-start | bytes 11528 | tf_op jit(solution)/shard_map/ppermute | solution.py:36
  16.3 9.3 %collective-permute-start = (bf16[3,2,320]{2,1,0:T(2,128)(2,1)S(1)}, bf16[3,2,320]{2,1,0:T(2,128)(2,1)S(1)}, u32[]{:S(2)}, u32[]{:S(2)}) collective-permute-start(bf16[3,2,320]{2,1,0:T(2,128)(2,1)S(1)} %get-tuple-element.27), channel_id=1, source_target_pairs={{0,4},{4,8},{8,12},{1,5},{5,9},{9,13},{2,6},{6,10},{10,14},{3,7},{... | collective-permute-start | bytes 11528 | tf_op jit(solution)/shard_map/ppermute | solution.py:34
  25.5 88.8 %reduce-scatter.9.cloned.1.call-start = ((), (), s32[]{:S(2)}) async-start(), calls=%async_computation.4 | async-start | bytes 2949120 | tf_op jit(solution)/shard_map/reduce_scatter | solution.py:59
  63.3 0.7 copy-start.4
  63.3 51.1 %copy-start.2 = (s32[3,64,512]{2,1,0:T(8,128)S(1)}, s32[3,64,512]{2,1,0:T(8,128)}, u32[]{:S(2)}) copy-start(s32[3,64,512]{2,1,0:T(8,128)} %param.11) | copy-start | bytes 1179652
  63.3 139.6 %reduce-scatter.11.cloned.1.call-start = ((), (), s32[]{:S(2)}) async-start(), calls=%async_computation.6 | async-start | bytes 1966080 | tf_op jit(solution)/shard_map/reduce_scatter | solution.py:72
  65.0 51.7 %copy-start.1 = (bf16[512,1536]{1,0:T(8,128)(2,1)S(1)}, bf16[512,1536]{1,0:T(8,128)(2,1)}, u32[]{:S(2)}) copy-start(bf16[512,1536]{1,0:T(8,128)(2,1)} %all-gather.2.cloned.1.call-done) | copy-start | bytes 4718596
  117.1 14.9 %collective-permute-start.2 = (bf16[1,3,64,1536]{3,2,1,0:T(8,128)(2,1)S(1)}, bf16[1,3,64,1536]{3,2,1,0:T(8,128)(2,1)}, u32[]{:S(2)}, u32[]{:S(2)}) collective-permute-start(bf16[1,3,64,1536]{3,2,1,0:T(8,128)(2,1)S(1)} %fusion.12), channel_id=1, source_target_pairs={{0,1},{1,0},{2,3},{3,2},{4,5},{5,4},{6,7},{7,6},{8,9},{9,8},{10,11... | collective-permute-start | bytes 1769480 | tf_op jit(solution)/shard_map/ppermute | solution.py:19
  120.9 157.7 %reduce-scatter.15.cloned.1.call-start = ((), (), s32[]{:S(2)}) async-start(), calls=%async_computation.8 | async-start | bytes 491520
  133.2 52.8 %collective-permute-start.3 = (bf16[2,3,64,1536]{3,2,1,0:T(8,128)(2,1)S(1)}, bf16[2,3,64,1536]{3,2,1,0:T(8,128)(2,1)}, u32[]{:S(2)}, u32[]{:S(2)}) collective-permute-start(bf16[2,3,64,1536]{3,2,1,0:T(8,128)(2,1)S(1)} %pad_maximum_fusion.2), channel_id=1, source_target_pairs={{0,2},{1,3},{2,0},{3,1},{4,6},{5,7},{6,4},{7,5},{8,10},{9,11},{10,... | collective-permute-start | bytes 3538952 | tf_op jit(solution)/shard_map/ppermute | solution.py:19
  204.9 87.7 %reduce-scatter.13.cloned.1.call-start = ((), (), s32[]{:S(2)}) async-start(), calls=%async_computation.7 | async-start | bytes 6389760
  242.1 2.6 collective-permute-start.4
  243.4 4.9 %collective-permute-start.5 = (bf16[3,1,1536]{2,1,0:T(2,128)(2,1)S(1)}, bf16[3,1,1536]{2,1,0:T(2,128)(2,1)S(1)}, u32[]{:S(2)}, u32[]{:S(2)}) collective-permute-start(bf16[3,1,1536]{2,1,0:T(2,128)(2,1)S(1)} %get-tuple-element.15), channel_id=1, source_target_pairs={{4,0},{8,4},{12,8},{5,1},{9,5},{13,9},{6,2},{10,6},{14,10},{7,3},{... | collective-permute-start | bytes 27656 | tf_op jit(solution)/shard_map/ppermute | solution.py:36
  259.7 15.3 %copy-start = (f32[3,512,320]{2,1,0:T(8,128)S(1)}, f32[3,512,320]{2,1,0:T(8,128)}, u32[]{:S(2)}) copy-start(f32[3,512,320]{2,1,0:T(8,128)} %get-tuple-element.13) | copy-start | bytes 5898244
Sparse Core Ops, SparseCore 0:
  25.6 39.3 all-gather.1
  67.3 47.0 reduce-scatter.8
  121.0 28.0 reduce-scatter.10
  205.0 20.6 reduce-scatter.14
  242.1 50.3 reduce-scatter.12
